TPU v7x, 256 devices: a whole 4x4x8 slice. The times are simulated.
256 devices in a mesh: ep: 64 (over y, z, core), dp: 4 (over x).
Axes of the slice: x: 4, y: 4, z: 8, core: 2. Of those that a mesh axis runs over, the one named last changes fastest.
Arguments:
- tokens: bfloat16 [8192, 2048], P(('ep', 'dp')), may hold values from -6 to 6
- cotangent: bfloat16 [8192, 2048], P(('ep', 'dp')), may hold values from -6 to 6
- expert_ids: int32 [8192, 8], P(('ep', 'dp')), may hold values from 0 to 63, as said below
- route_weights: bfloat16 [8192, 8], P(('ep', 'dp')), may hold values from 0.049804688 to 0.5
- w_gate: bfloat16 [64, 2048, 768], P('ep'), may hold values from -0.125 to 0.125
- w_up: bfloat16 [64, 2048, 768], P('ep'), may hold values from -0.125 to 0.125
- w_down: bfloat16 [64, 768, 2048], P('ep'), may hold values from -0.21875 to 0.21875
Outputs:
- grad_tokens: bfloat16 [8192, 2048], P(('ep', 'dp'))
- grad_route: bfloat16 [8192, 8], P(('ep', 'dp'))
- grad_gate: bfloat16 [64, 2048, 768], P('ep', 'dp')
- grad_up: bfloat16 [64, 2048, 768], P('ep', 'dp')
- grad_down: bfloat16 [64, 768, 2048], P('ep', None, 'dp')
Inputs may be any that keep to these rules, and one draw needn't show every extreme that they name: `expert_ids`: each token names 8 different experts. The tokens of one device name no expert more than 8 times; 4 experts, drawn from the seed, are named exactly 8 times by every device's tokens.
All inputs are finite; a program needn't handle non-finite values.
Results may differ from a plain program's by a relative error of at most 0.0095.
Values may be sent and summed in bfloat16 or wider, within the bound.
No kernel may reach another device: no remote copies, remote signals or barrier semaphores. Data moves between devices by JAX's collectives and lax.ppermute only.
A program may use at most 128 MiB of HBM per device.

v0:
```python
import jax
import jax.numpy as jnp
from jax import lax
from jax.sharding import PartitionSpec as P

block_rows = 128
contract_last = (((1,), (1,)), ((), ()))
contract_first = (((0,), (0,)), ((), ()))


def silu_parts(gate_pre):
    sig = jax.nn.sigmoid(gate_pre)
    return (gate_pre * sig, sig * (1.0 + gate_pre * (1.0 - sig)))


def expert_pass(rows_x, rows_cot, rows_w, live_count, w_gate_one, w_up_one, w_down_one):
    total, model = rows_x.shape
    width = w_gate_one.shape[1]

    def step(index, carry):
        acc_gate, acc_up, acc_down, slot_grad, route_grad = carry
        start = index * block_rows
        tok = lax.dynamic_slice_in_dim(rows_x, start, block_rows, 0)
        cot = lax.dynamic_slice_in_dim(rows_cot, start, block_rows, 0)
        weight = lax.dynamic_slice_in_dim(rows_w, start, block_rows, 0).astype(jnp.float32)[:, None]
        gate_pre = jnp.dot(tok, w_gate_one, preferred_element_type=jnp.float32)
        up_pre = jnp.dot(tok, w_up_one, preferred_element_type=jnp.float32)
        act, slope = silu_parts(gate_pre)
        hidden = lax.optimization_barrier((act * up_pre).astype(jnp.bfloat16))
        back = lax.dot_general(cot, w_down_one, contract_last, preferred_element_type=jnp.float32)
        route_part = jnp.sum(hidden.astype(jnp.float32) * back, axis=1)
        scaled = weight * back
        grad_gate_pre = (scaled * up_pre * slope).astype(jnp.bfloat16)
        grad_up_pre = (scaled * act).astype(jnp.bfloat16)
        scaled_cot = (weight * cot.astype(jnp.float32)).astype(jnp.bfloat16)
        part = lax.dot_general(
            grad_gate_pre, w_gate_one, contract_last, preferred_element_type=jnp.float32
        )
        part = part + lax.dot_general(
            grad_up_pre, w_up_one, contract_last, preferred_element_type=jnp.float32
        )
        acc_gate = acc_gate + lax.dot_general(
            tok, grad_gate_pre, contract_first, preferred_element_type=jnp.float32
        )
        acc_up = acc_up + lax.dot_general(
            tok, grad_up_pre, contract_first, preferred_element_type=jnp.float32
        )
        acc_down = acc_down + lax.dot_general(
            hidden, scaled_cot, contract_first, preferred_element_type=jnp.float32
        )
        slot_grad = lax.dynamic_update_slice_in_dim(slot_grad, part, start, 0)
        route_grad = lax.dynamic_update_slice_in_dim(route_grad, route_part, start, 0)
        return (acc_gate, acc_up, acc_down, slot_grad, route_grad)

    init = (
        jnp.zeros((model, width), jnp.float32),
        jnp.zeros((model, width), jnp.float32),
        jnp.zeros((width, model), jnp.float32),
        jnp.zeros((total, model), jnp.float32),
        jnp.zeros((total,), jnp.float32),
    )
    block_count = (live_count + block_rows - 1) // block_rows
    return lax.fori_loop(0, block_count, step, init)


def body(tokens, cotangent, expert_ids, route_weights, w_gate, w_up, w_down):
    tok_count, topk = expert_ids.shape
    model = tokens.shape[1]
    experts = lax.axis_size("ep")
    capacity = min(tok_count, 2 * tok_count * topk // experts)
    slots = tok_count * topk
    row_total = experts * capacity
    flat_ids = expert_ids.reshape(slots)
    onehot = (flat_ids[:, None] == jnp.arange(experts, dtype=jnp.int32)[None, :]).astype(jnp.int32)
    position = jnp.sum((jnp.cumsum(onehot, axis=0) - 1) * onehot, axis=1)
    slot_ids = jnp.arange(slots, dtype=jnp.int32)
    source = (
        jnp.full((row_total,), slots, jnp.int32).at[flat_ids * capacity + position].set(slot_ids)
    )
    filled = source < slots
    source_token = jnp.where(filled, source // topk, tok_count)
    joined = jnp.concatenate([tokens, cotangent], axis=1)
    picked = jnp.take(joined, source_token, axis=0, mode="fill", fill_value=0)
    send_x = picked[:, :model].reshape(experts, capacity, model)
    send_cot = picked[:, model:].reshape(experts, capacity, model)
    send_w = jnp.take(
        route_weights.reshape(slots), jnp.where(filled, source, slots), mode="fill", fill_value=0
    ).reshape(experts, capacity)
    recv_x, recv_cot, recv_w = (
        lax.all_to_all(send_x, "ep", split_axis=0, concat_axis=0, tiled=True),
        lax.all_to_all(send_cot, "ep", split_axis=0, concat_axis=0, tiled=True),
        lax.all_to_all(send_w, "ep", split_axis=0, concat_axis=0, tiled=True),
    )
    flat_w = recv_w.reshape(row_total)
    live = (flat_w != 0).astype(jnp.int32)
    live_count = jnp.sum(live)
    place = jnp.where(live > 0, jnp.cumsum(live) - 1, row_total)
    anchor = (
        jnp.full((row_total,), row_total, jnp.int32)
        .at[place]
        .set(jnp.arange(row_total, dtype=jnp.int32), mode="drop")
    )
    recv_joined = jnp.concatenate(
        [recv_x.reshape(row_total, model), recv_cot.reshape(row_total, model)], axis=1
    )
    packed = jnp.take(recv_joined, anchor, axis=0, mode="fill", fill_value=0)
    pack_x = packed[:, :model]
    pack_cot = packed[:, model:]
    pack_w = jnp.take(flat_w, anchor, mode="fill", fill_value=0)
    w_gate_one = w_gate[0]
    w_up_one = w_up[0]
    w_down_one = w_down[0]
    acc_gate, acc_up, acc_down, slot_grad, route_grad = expert_pass(
        pack_x, pack_cot, pack_w, live_count, w_gate_one, w_up_one, w_down_one
    )
    slot_rows = jnp.take(slot_grad, place, axis=0, mode="fill", fill_value=0.0).astype(jnp.bfloat16)
    route_rows = jnp.take(route_grad, place, axis=0, mode="fill", fill_value=0.0).astype(
        jnp.bfloat16
    )
    back_x, back_route_rows = (
        lax.all_to_all(
            slot_rows.reshape(experts, capacity, model),
            "ep",
            split_axis=0,
            concat_axis=0,
            tiled=True,
        ),
        lax.all_to_all(
            route_rows.reshape(experts, capacity), "ep", split_axis=0, concat_axis=0, tiled=True
        ),
    )
    mine_rows = back_x[flat_ids, position].reshape(tok_count, topk, model)
    grad_tokens = jnp.sum(mine_rows.astype(jnp.float32), axis=1).astype(jnp.bfloat16)
    grad_route = back_route_rows[flat_ids, position].reshape(tok_count, topk)
    summed = (
        lax.psum_scatter(
            acc_gate[None].astype(jnp.bfloat16), "dp", scatter_dimension=1, tiled=True
        ).astype(jnp.float32),
        lax.psum_scatter(
            acc_up[None].astype(jnp.bfloat16), "dp", scatter_dimension=1, tiled=True
        ).astype(jnp.float32),
        lax.psum_scatter(
            acc_down[None].astype(jnp.bfloat16), "dp", scatter_dimension=2, tiled=True
        ).astype(jnp.float32),
    )
    return (
        grad_tokens,
        grad_route,
        summed[0].astype(jnp.bfloat16),
        summed[1].astype(jnp.bfloat16),
        summed[2].astype(jnp.bfloat16),
    )


def solution(mesh):
    return jax.shard_map(
        body,
        mesh=mesh,
        in_specs=(
            P(("ep", "dp"), None),
            P(("ep", "dp"), None),
            P(("ep", "dp"), None),
            P(("ep", "dp"), None),
            P("ep", None, None),
            P("ep", None, None),
            P("ep", None, None),
        ),
        out_specs=(
            P(("ep", "dp"), None),
            P(("ep", "dp"), None),
            P("ep", "dp", None),
            P("ep", "dp", None),
            P("ep", None, "dp"),
        ),
        check_vma=False,
    )
```

profile of v0, /device:TPU:1, one launch (start us, length us, event | category | flops | bytes accessed | tf_op | source)
XLA Modules:
  0.0 412.4 jit_solution(326719963543742656)
XLA Ops:
  12.0 3.4 gather_fusion
  16.1 13.2 %all-to-all-start = ((bf16[64,1,8]{2,1,0:T(2,128)(2,1)}), bf16[64,1,8]{2,1,0:T(2,128)(2,1)S(1)}, u32[]{:S(2)}, u32[]{:S(2)}) async-start(bf16[64,1,8]{2,1,0:T(2,128)(2,1)} %select_n.173), calls=%async_computation | async-start | bytes 65536 | tf_op jit(solution)/shard_map/all_to_all | solution.py:92
  30.3 4.4 %gather_fusion.1 = bf16[512,4096]{1,0:T(8,128)(2,1)} fusion(bf16[32,4096]{1,0:T(8,128)(2,1)S(1)} %pad_maximum_fusion.1, s32[1024]{0:T(1024)S(1)} %pad_clamp_fusion.2), kind=kCustom, calls=%fused_computation.1 | custom fusion | bytes 8390656 | tf_op jit(solution)/shard_map/jit(_take)/gather | solution.py:83
  39.7 61.6 %all_to_all.30 = bf16[64,8,2048]{2,1,0:T(8,128)(2,1)S(1)} all-to-all(bf16[64,8,2048]{2,1,0:T(8,128)(2,1)} %get-tuple-element.145), channel_id=1, replica_groups=mesh['ep'=64,'dp'=4] {'ep'}, dimensions={0} | all-to-all | bytes 4194304 | tf_op jit(solution)/shard_map/all_to_all | solution.py:90
  101.3 6.0 %all-to-all-start.2 = ((bf16[64,8,2048]{2,1,0:T(8,128)(2,1)}), bf16[64,8,2048]{2,1,0:T(8,128)(2,1)}, u32[]{:S(2)}, u32[]{:S(2)}) async-start(bf16[64,8,2048]{2,1,0:T(8,128)(2,1)} %get-tuple-element.146), calls=%async_computation.2 | async-start | bytes 4194304 | tf_op jit(solution)/shard_map/all_to_all | solution.py:91
  112.9 3.5 gather_fusion.3
  116.5 42.0 %all-to-all-done.2 = bf16[64,8,2048]{2,1,0:T(8,128)(2,1)} async-done(((bf16[64,8,2048]{2,1,0:T(8,128)(2,1)}), bf16[64,8,2048]{2,1,0:T(8,128)(2,1)}, u32[]{:S(2)}, u32[]{:S(2)}) %all-to-all-start.2) | async-done | bytes 2097184 | tf_op jit(solution)/shard_map/all_to_all | solution.py:91
  158.4 3.9 pad_maximum_fusion
  162.4 11.3 %gather_fusion.2 = bf16[512,4096]{1,0:T(8,128)(2,1)} fusion(bf16[512,4096]{1,0:T(8,128)(2,1)} %pad_maximum_fusion, s32[1024]{0:T(1024)S(1)} %pad_clamp_fusion.1), kind=kCustom, calls=%fused_computation.2 | custom fusion | bytes 8390656 | tf_op jit(solution)/shard_map/jit(_take)/gather | solution.py:106
  178.8 3.0 broadcast.268
  181.8 3.1 broadcast.268.clone
  184.9 3.4 broadcast_in_dim.91
  189.8 65.8 %while.18 = (s32[]{:T(128)}, f32[2048,768]{1,0:T(8,128)}, f32[2048,768]{1,0:T(8,128)}, f32[768,2048]{1,0:T(8,128)}, bf16[512,2048]{1,0:T(8,128)(2,1)}, /*index=5...) while((s32[]{:T(128)}, f32[2048,768]{1,0:T(8,128)}, ...), condition=%wide.region_10.11_spmd, body=%wide.region_8.10_spmd.sunk | while | flops 3228860416 | bytes 254741648 | solution.py:63
  255.7 4.8 %convert_bitcast_fusion.2 = bf16[1,2048,768]{2,1,0:T(8,128)(2,1)} fusion(f32[2048,768]{1,0:T(8,128)} %get-tuple-element.79), kind=kLoop, calls=%fused_computation.46 | loop fusion | flops 1572864 | bytes 9437184 | tf_op jit(solution)/shard_map/convert_element_type | solution.py:137
  260.5 4.7 %convert_bitcast_fusion.1 = bf16[1,2048,768]{2,1,0:T(8,128)(2,1)} fusion(f32[2048,768]{1,0:T(8,128)} %get-tuple-element.80), kind=kLoop, calls=%fused_computation.45 | loop fusion | flops 1572864 | bytes 9437184 | tf_op jit(solution)/shard_map/convert_element_type | solution.py:140
  265.3 4.9 %convert_bitcast_fusion = bf16[1,768,2048]{2,1,0:T(8,128)(2,1)} fusion(f32[768,2048]{1,0:T(8,128)} %get-tuple-element.81), kind=kLoop, calls=%fused_computation.44 | loop fusion | flops 1572864 | bytes 9437184 | tf_op jit(solution)/shard_map/convert_element_type | solution.py:143
  270.5 3.5 gather_fusion.6
  275.0 26.3 %all-to-all-start.4 = ((bf16[64,1,8]{2,1,0:T(2,128)(2,1)}), bf16[64,1,8]{2,1,0:T(2,128)(2,1)S(1)}, u32[]{:S(2)}, u32[]{:S(2)}) async-start(bf16[64,1,8]{2,1,0:T(2,128)(2,1)} %copy.61), calls=%async_computation.4 | async-start | bytes 65536 | tf_op jit(solution)/shard_map/all_to_all | solution.py:128
  301.3 3.3 gather_fusion.4
  304.7 3.4 fusion.18
  310.6 7.9 %all-to-all-start.3 = ((bf16[64,8,2048]{2,1,0:T(8,128)(2,1)}), bf16[64,8,2048]{2,1,0:T(8,128)(2,1)S(1)}, u32[]{:S(2)}, u32[]{:S(2)}) async-start(bf16[64,8,2048]{2,1,0:T(8,128)(2,1)} %fusion.18), calls=%async_computation.3 | async-start | bytes 4194304 | tf_op jit(solution)/shard_map/all_to_all | solution.py:121
  321.7 48.0 %all-to-all-done.3 = bf16[64,8,2048]{2,1,0:T(8,128)(2,1)S(1)} async-done(((bf16[64,8,2048]{2,1,0:T(8,128)(2,1)}), bf16[64,8,2048]{2,1,0:T(8,128)(2,1)S(1)}, u32[]{:S(2)}, u32[]{:S(2)}) %all-to-all-start.3) | async-done | bytes 2097184 | tf_op jit(solution)/shard_map/all_to_all | solution.py:121
  369.7 4.3 %gather_fusion.5 = bf16[256,2048]{1,0:T(8,128)(2,1)S(1)} fusion(bf16[64,8,2048]{2,1,0:T(8,128)(2,1)S(1)} %all-to-all-done.3, s32[256]{0:T(256)S(1)} %bitcast.90), kind=kCustom, calls=%fused_computation.5 | custom fusion | bytes 2099200 | tf_op jit(solution)/shard_map/gather | solution.py:132
  375.4 30.5 %reduce-scatter.8.cloned.1.call-done = bf16[1,768,512]{2,1,0:T(8,128)(2,1)} async-done(((bf16[1,768,2048]{2,1,0:T(8,128)(2,1)}), bf16[1,768,512]{2,1,0:T(8,128)(2,1)}) %reduce-scatter.8.cloned.1.call-update) | async-done | bytes 786448 | tf_op jit(solution)/shard_map/reduce_scatter | solution.py:142
  (214 shorter events, 96.8 us)
Async XLA Ops:
  16.1 23.6 %all-to-all-start = ((bf16[64,1,8]{2,1,0:T(2,128)(2,1)}), bf16[64,1,8]{2,1,0:T(2,128)(2,1)S(1)}, u32[]{:S(2)}, u32[]{:S(2)}) async-start(bf16[64,1,8]{2,1,0:T(2,128)(2,1)} %select_n.173), calls=%async_computation | async-start | bytes 65536 | tf_op jit(solution)/shard_map/all_to_all | solution.py:92
  101.3 57.2 %all-to-all-start.2 = ((bf16[64,8,2048]{2,1,0:T(8,128)(2,1)}), bf16[64,8,2048]{2,1,0:T(8,128)(2,1)}, u32[]{:S(2)}, u32[]{:S(2)}) async-start(bf16[64,8,2048]{2,1,0:T(8,128)(2,1)} %get-tuple-element.146), calls=%async_computation.2 | async-start | bytes 4194304 | tf_op jit(solution)/shard_map/all_to_all | solution.py:91
  107.3 268.1 %reduce-scatter.4.cloned.1.call-start = ((), (), s32[]{:S(2)}) async-start(), calls=%async_computation.8 | async-start | bytes 3932160 | tf_op jit(solution)/shard_map/reduce_scatter | solution.py:136
  184.9 5.0 %copy-start = (bf16[1,2048,768]{2,1,0:T(8,128)(2,1)S(1)}, bf16[1,2048,768]{2,1,0:T(8,128)(2,1)}, u32[]{:S(2)}) copy-start(bf16[1,2048,768]{2,1,0:T(8,128)(2,1)} %param.14) | copy-start | bytes 9437188
  189.8 4.3 %copy-start.11 = (bf16[768,2048]{1,0:T(8,128)(2,1)S(1)}, bf16[768,2048]{1,0:T(8,128)(2,1)}, u32[]{:S(2)}) copy-start(bf16[768,2048]{1,0:T(8,128)(2,1)} %get-tuple-element.281) | copy-start | bytes 9437188 | tf_op jit(solution)/shard_map/while
  189.9 5.5 %slice-start.4 = ((s8[6291456]{0:T(1024)(128)(4,1)}), s8[4194304]{0:T(1024)(128)(4,1)S(1)}, s32[]{:S(2)}) async-start(s8[6291456]{0:T(1024)(128)(4,1)} %bitcast.86), calls=%async_computation.15 | async-start | bytes 8388608 | tf_op jit(solution)/shard_map/while
  195.4 4.5 %slice-start.2 = ((s8[6291456]{0:T(1024)(128)(4,1)}), s8[4194304]{0:T(1024)(128)(4,1)S(1)}, s32[]{:S(2)}) async-start(s8[6291456]{0:T(1024)(128)(4,1)} %bitcast.84), calls=%async_computation.13 | async-start | bytes 8388608 | tf_op jit(solution)/shard_map/while
  199.9 4.2 %slice-start.1 = ((s8[6291456]{0:T(1024)(128)(4,1)}), s8[2097152]{0:T(1024)(128)(4,1)S(1)}, s32[]{:S(2)}) async-start(s8[6291456]{0:T(1024)(128)(4,1)} %bitcast.82), calls=%async_computation.12 | async-start | bytes 4194304 | tf_op jit(solution)/shard_map/while
  206.0 4.3 %copy-start.2 = (f32[2048,768]{1,0:T(8,128)}, f32[2048,768]{1,0:T(8,128)S(1)}, u32[]{:S(2)}) copy-start(f32[2048,768]{1,0:T(8,128)S(1)} %convolution_add_fusion.7) | copy-start | bytes 18874372 | tf_op jit(solution)/shard_map/while
  211.8 4.3 %copy-start.11 = (bf16[768,2048]{1,0:T(8,128)(2,1)S(1)}, bf16[768,2048]{1,0:T(8,128)(2,1)}, u32[]{:S(2)}) copy-start(bf16[768,2048]{1,0:T(8,128)(2,1)} %get-tuple-element.281) | copy-start | bytes 9437188 | tf_op jit(solution)/shard_map/while
  211.8 5.5 %slice-start.4 = ((s8[6291456]{0:T(1024)(128)(4,1)}), s8[4194304]{0:T(1024)(128)(4,1)S(1)}, s32[]{:S(2)}) async-start(s8[6291456]{0:T(1024)(128)(4,1)} %bitcast.86), calls=%async_computation.15 | async-start | bytes 8388608 | tf_op jit(solution)/shard_map/while
  217.3 4.5 %slice-start.2 = ((s8[6291456]{0:T(1024)(128)(4,1)}), s8[4194304]{0:T(1024)(128)(4,1)S(1)}, s32[]{:S(2)}) async-start(s8[6291456]{0:T(1024)(128)(4,1)} %bitcast.84), calls=%async_computation.13 | async-start | bytes 8388608 | tf_op jit(solution)/shard_map/while
  221.9 4.2 %slice-start.1 = ((s8[6291456]{0:T(1024)(128)(4,1)}), s8[2097152]{0:T(1024)(128)(4,1)S(1)}, s32[]{:S(2)}) async-start(s8[6291456]{0:T(1024)(128)(4,1)} %bitcast.82), calls=%async_computation.12 | async-start | bytes 4194304 | tf_op jit(solution)/shard_map/while
  227.9 4.3 %copy-start.2 = (f32[2048,768]{1,0:T(8,128)}, f32[2048,768]{1,0:T(8,128)S(1)}, u32[]{:S(2)}) copy-start(f32[2048,768]{1,0:T(8,128)S(1)} %convolution_add_fusion.7) | copy-start | bytes 18874372 | tf_op jit(solution)/shard_map/while
  233.7 4.3 %copy-start.11 = (bf16[768,2048]{1,0:T(8,128)(2,1)S(1)}, bf16[768,2048]{1,0:T(8,128)(2,1)}, u32[]{:S(2)}) copy-start(bf16[768,2048]{1,0:T(8,128)(2,1)} %get-tuple-element.281) | copy-start | bytes 9437188 | tf_op jit(solution)/shard_map/while
  233.7 5.5 %slice-start.4 = ((s8[6291456]{0:T(1024)(128)(4,1)}), s8[4194304]{0:T(1024)(128)(4,1)S(1)}, s32[]{:S(2)}) async-start(s8[6291456]{0:T(1024)(128)(4,1)} %bitcast.86), calls=%async_computation.15 | async-start | bytes 8388608 | tf_op jit(solution)/shard_map/while
  239.3 4.5 %slice-start.2 = ((s8[6291456]{0:T(1024)(128)(4,1)}), s8[4194304]{0:T(1024)(128)(4,1)S(1)}, s32[]{:S(2)}) async-start(s8[6291456]{0:T(1024)(128)(4,1)} %bitcast.84), calls=%async_computation.13 | async-start | bytes 8388608 | tf_op jit(solution)/shard_map/while
  249.8 4.3 %copy-start.2 = (f32[2048,768]{1,0:T(8,128)}, f32[2048,768]{1,0:T(8,128)S(1)}, u32[]{:S(2)}) copy-start(f32[2048,768]{1,0:T(8,128)S(1)} %convolution_add_fusion.7) | copy-start | bytes 18874372 | tf_op jit(solution)/shard_map/while
  260.5 114.9 %reduce-scatter.6.cloned.1.call-start = ((), (), s32[]{:S(2)}) async-start(), calls=%async_computation.9 | async-start | bytes 3932160 | tf_op jit(solution)/shard_map/reduce_scatter | solution.py:139
  265.3 140.6 %reduce-scatter.8.cloned.1.call-start = ((), (), s32[]{:S(2)}) async-start(), calls=%async_computation.10 | async-start | bytes 3932160 | tf_op jit(solution)/shard_map/reduce_scatter | solution.py:142
  270.2 31.1 %copy-start.7 = (bf16[512,2048]{1,0:T(8,128)(2,1)S(1)}, bf16[512,2048]{1,0:T(8,128)(2,1)}, u32[]{:S(2)}) copy-start(bf16[512,2048]{1,0:T(8,128)(2,1)} %get-tuple-element.77) | copy-start | bytes 6291460
  275.0 35.6 %all-to-all-start.4 = ((bf16[64,1,8]{2,1,0:T(2,128)(2,1)}), bf16[64,1,8]{2,1,0:T(2,128)(2,1)S(1)}, u32[]{:S(2)}, u32[]{:S(2)}) async-start(bf16[64,1,8]{2,1,0:T(2,128)(2,1)} %copy.61), calls=%async_computation.4 | async-start | bytes 65536 | tf_op jit(solution)/shard_map/all_to_all | solution.py:128
  308.1 10.5 %copy-start.9 = (s32[256,1]{0,1:T(1,128)S(1)}, s32[256,1]{0,1:T(1,128)}, u32[]{:S(2)}) copy-start(s32[256,1]{0,1:T(1,128)} %get-tuple-element.147) | copy-start | bytes 3076
  310.6 59.2 %all-to-all-start.3 = ((bf16[64,8,2048]{2,1,0:T(8,128)(2,1)}), bf16[64,8,2048]{2,1,0:T(8,128)(2,1)S(1)}, u32[]{:S(2)}, u32[]{:S(2)}) async-start(bf16[64,8,2048]{2,1,0:T(8,128)(2,1)} %fusion.18), calls=%async_computation.3 | async-start | bytes 4194304 | tf_op jit(solution)/shard_map/all_to_all | solution.py:121
  (31 other events, 92.0 us)
Sparse Core Ops, SparseCore 0:
  260.6 57.8 reduce-scatter.3
  321.6 40.5 reduce-scatter.5
  365.3 40.5 reduce-scatter.7
where the time goes:
time: 414 us; the launch traced here: 412 us
  waiting for transfers between devices  123 us (30%)
  local copies, waits for them, and re-layouts  94.7 us (23%)
  blocking collectives  61.6 us (15%)
  starting transfers between devices  53.6 us (13%)
  other arithmetic  32.4 us (8%)
  matrix products  32 us (8%)
  between operations  14.7 us (4%)
    all_to_all x1, blocking collectives, body(): lax.all_to_all(send_x, 'ep', split_axis=0, concat_axis=0, tiled=True)  61.6 us
    all_to_all x1, waiting for transfers between devices, body(): lax.all_to_all(slot_rows.reshape(experts, capacity, model), 'ep', split_a...  48 us
    all_to_all x1, waiting for transfers between devices, body(): lax.all_to_all(send_cot, 'ep', split_axis=0, concat_axis=0, tiled=True)  42 us
    while x90, local copies, waits for them, and re-layouts  32.2 us
    reduce_scatter x1, waiting for transfers between devices, body(): lax.psum_scatter(acc_down[None].astype(jnp.bfloat16), 'dp', scatter_dimen...  30.5 us
    all_to_all x1, starting transfers between devices, body(): lax.all_to_all(route_rows.reshape(experts, capacity), 'ep', split_axis=0,...  26.3 us
    all_to_all x1, starting transfers between devices, body(): lax.all_to_all(send_w, 'ep', split_axis=0, concat_axis=0, tiled=True)  13.2 us
    gather x1, local copies, waits for them, and re-layouts, body(): packed = jnp.take(recv_joined, anchor, axis=0, mode='fill', fill_value=0)  11.3 us
  transfers between devices with their start and end apart: 7, of which 4 were waited for; matrix products, arithmetic and copies ran while one was open for 12% of the time, Pallas kernels for 0%

commit v1 on v0

v1 whole, which is shorter than its diff:
```python
import jax
import jax.numpy as jnp
from jax import lax
from jax.experimental import pallas as pl
from jax.experimental.pallas import tpu as pltpu
from jax.sharding import PartitionSpec as P

bf16 = jnp.bfloat16
f32 = jnp.float32
i32 = jnp.int32

NY, NZ, NC = 4, 8, 2
CAP = 8
TOK = 32
TOPK = 8
D = 2048
FF = 768
META = 128
DA = D + META
HALF = NY * NZ * CAP
ROWS = 2 * HALF
FB = 256
NFB = FF // FB
DY = (0, -1, 1, 2)
DZ = (0, -1, -2, -3, 4, 1, 2, 3)
VLIM = 60 * 1024 * 1024

contract_last = (((1,), (1,)), ((), ()))
contract_first = (((0,), (0,)), ((), ()))
nothing = (((1,), (0,)), ((), ()))


def dot(a, b, dims=nothing):
    return lax.dot_general(a, b, dims, preferred_element_type=f32)


def flat(y, z, c):
    return ((y % NY) * NZ + (z % NZ)) * NC + c


def shift(arr, dy=0, dz=0):
    pairs = [
        (flat(y, z, c), flat(y + dy, z + dz, c))
        for y in range(NY)
        for z in range(NZ)
        for c in range(NC)
    ]
    return lax.ppermute(arr, "ep", pairs)


def swap_core(arr):
    return lax.ppermute(arr, "ep", [(i, i ^ 1) for i in range(NY * NZ * NC)])


VM = pl.BlockSpec(memory_space=pltpu.VMEM)
SM = pl.BlockSpec(memory_space=pltpu.SMEM)


def iota(shape, dim):
    return lax.broadcasted_iota(i32, shape, dim)


def pick_x_kernel(me_ref, b0, b1, b2, b3a, b3b, own_ref, sib_ref, code_ref):
    me = me_ref[0]
    n = NZ * TOK
    lane = iota((n, META), 1)
    tok = iota((n, META), 0)
    expert = jnp.where(lane < 64, me, me ^ 1).astype(f32)
    low = iota((n, n), 0)
    col = iota((n, n), 1)
    before = jnp.where((col < low) & (col // TOK == low // TOK), 1.0, 0.0).astype(bf16)
    row_pos = (lane % CAP).astype(f32)
    row_src = (lane % 64) // CAP
    for b in range(NY):
        if b < 3:
            blk = (b0, b1, b2)[b][...]
        else:
            blk = jnp.concatenate([b3a[...], b3b[...]], axis=0)
        meta = blk[:, D:].astype(f32)
        named = jnp.zeros((n, META), f32)
        for k in range(TOPK):
            ident = jnp.broadcast_to(meta[:, k : k + 1], (n, META))
            named = jnp.where(ident == expert, 1.0, named)
        earlier = dot(before, named.astype(bf16))
        code = jnp.where(named > 0, earlier, -1.0)
        code_ref[b] = code.astype(bf16)
        sel = jnp.where((code == row_pos) & (tok // TOK == row_src), 1.0, 0.0).astype(bf16)
        rows = dot(sel, blk, contract_first).astype(bf16)
        own_ref[b * 64 : (b + 1) * 64, :] = rows[:64]
        sib_ref[b * 64 : (b + 1) * 64, :] = rows[64:]


def pick_x(me, blocks):
    return pl.pallas_call(
        pick_x_kernel,
        out_shape=(
            jax.ShapeDtypeStruct((HALF, DA), bf16),
            jax.ShapeDtypeStruct((HALF, DA), bf16),
            jax.ShapeDtypeStruct((NY, NZ * TOK, META), bf16),
        ),
        in_specs=[SM] + [VM] * 5,
        out_specs=(VM, VM, VM),
        compiler_params=pltpu.CompilerParams(vmem_limit_bytes=VLIM),
        name="pick_x",
    )(me, *blocks)


def pick_cot_kernel(code_ref, *refs):
    blocks = refs[:9]
    own_ref, sib_ref, own_acc, sib_acc = refs[9:]
    n = NY * TOK
    lane = iota((n, META), 1)
    tok = iota((n, META), 0)
    row_pos = (lane % CAP).astype(f32)
    row_src = (lane % 64) // CAP
    place = 0
    for s in range(NZ):
        if DZ[s] == 4:
            blk = jnp.concatenate([blocks[place][...], blocks[place + 1][...]], axis=0)
            place += 2
        else:
            blk = blocks[place][...]
            place += 1
        code = jnp.concatenate(
            [code_ref[b, s * TOK : (s + 1) * TOK, :] for b in range(NY)], axis=0
        ).astype(f32)
        sel = jnp.where((code == row_pos) & (tok // TOK == row_src), 1.0, 0.0).astype(bf16)
        rows = dot(sel, blk, contract_first)
        for b in range(NY):
            at = b * 64 + s * CAP
            own_acc[at : at + CAP, :] = rows[b * CAP : (b + 1) * CAP]
            sib_acc[at : at + CAP, :] = rows[64 + b * CAP : 64 + (b + 1) * CAP]
    own_ref[...] = own_acc[...].astype(bf16)
    sib_ref[...] = sib_acc[...].astype(bf16)


def pick_cot(code, blocks):
    return pl.pallas_call(
        pick_cot_kernel,
        out_shape=(
            jax.ShapeDtypeStruct((HALF, D), bf16),
            jax.ShapeDtypeStruct((HALF, D), bf16),
        ),
        in_specs=[VM] * 10,
        out_specs=(VM, VM),
        scratch_shapes=[pltpu.VMEM((HALF, D), f32), pltpu.VMEM((HALF, D), f32)],
        compiler_params=pltpu.CompilerParams(vmem_limit_bytes=VLIM),
        name="pick_cot",
    )(code, *blocks)


def front_kernel(
    me_ref, own_ref, sib_ref, wg_ref, wu_ref,
    hid_ref, hid_t_ref, a_ref, b_ref, weight_ref, x_t_ref, x_scr,
):
    @pl.when(pl.program_id(0) == 0)
    def _():
        x_scr[:HALF] = own_ref[:, :D]
        x_scr[HALF:] = sib_ref[:, :D]
        x_t_ref[...] = x_scr[...].T
        meta = jnp.concatenate([own_ref[:, D:], sib_ref[:, D:]], axis=0).astype(f32)
        expert = me_ref[0].astype(f32)
        total = jnp.zeros((ROWS, 1), f32)
        for k in range(TOPK):
            total = total + jnp.where(
                meta[:, k : k + 1] == expert, meta[:, TOPK + k : TOPK + k + 1], 0.0
            )
        weight_ref[...] = jnp.broadcast_to(total, (ROWS, META))

    x = x_scr[...]
    gate = dot(x, wg_ref[...])
    up = dot(x, wu_ref[...])
    sig = jax.nn.sigmoid(gate)
    act = gate * sig
    hid = (act * up).astype(bf16)
    hid_ref[...] = hid
    hid_t_ref[...] = hid.T
    a_ref[...] = up * (sig * (1.0 + gate * (1.0 - sig)))
    b_ref[...] = act


def front(me, own, sib, wg, wu):
    whole = lambda shape: pl.BlockSpec(shape, lambda j: (0,) * len(shape))
    wide = pl.BlockSpec((ROWS, FB), lambda j: (0, j))
    return pl.pallas_call(
        front_kernel,
        grid=(NFB,),
        out_shape=(
            jax.ShapeDtypeStruct((ROWS, FF), bf16),
            jax.ShapeDtypeStruct((FF, ROWS), bf16),
            jax.ShapeDtypeStruct((ROWS, FF), f32),
            jax.ShapeDtypeStruct((ROWS, FF), f32),
            jax.ShapeDtypeStruct((ROWS, META), f32),
            jax.ShapeDtypeStruct((D, ROWS), bf16),
        ),
        in_specs=[
            SM, whole((HALF, DA)), whole((HALF, DA)),
            pl.BlockSpec((D, FB), lambda j: (0, j)),
            pl.BlockSpec((D, FB), lambda j: (0, j)),
        ],
        out_specs=(
            wide, pl.BlockSpec((FB, ROWS), lambda j: (j, 0)), wide, wide,
            whole((ROWS, META)), whole((D, ROWS)),
        ),
        scratch_shapes=[pltpu.VMEM((ROWS, D), bf16)],
        compiler_params=pltpu.CompilerParams(vmem_limit_bytes=VLIM),
        name="front",
    )(me, own, sib, wg, wu)


def grads_kernel(
    own_ref, sib_ref, hid_ref, hid_t_ref, a_ref, b_ref, weight_ref, x_t_ref, wd_ref,
    out_ref, gg_ref, gu_ref, route_ref, cot_scr, scot_scr,
):
    j = pl.program_id(0)

    @pl.when(j == 0)
    def _():
        cot_scr[:HALF] = own_ref[...]
        cot_scr[HALF:] = sib_ref[...]
        weight = weight_ref[:, :1]
        scot_scr[...] = (weight * cot_scr[...].astype(f32)).astype(bf16)
        route_ref[...] = jnp.zeros_like(route_ref)

    back = dot(cot_scr[...], wd_ref[...], contract_last)
    part = jnp.sum(hid_ref[...].astype(f32) * back, axis=1, keepdims=True)
    route_ref[...] += jnp.broadcast_to(part, (ROWS, META))
    scaled = weight_ref[:, :1] * back
    gg = (scaled * a_ref[...]).astype(bf16)
    gu = (scaled * b_ref[...]).astype(bf16)
    gg_ref[...] = gg
    gu_ref[...] = gu
    out_ref[:, :FB] = dot(x_t_ref[...], gg).astype(bf16)
    out_ref[:, FB : 2 * FB] = dot(x_t_ref[...], gu).astype(bf16)
    down = dot(hid_t_ref[...], scot_scr[...]).astype(bf16)
    for q in range(D // FB):
        out_ref[q * FB : (q + 1) * FB, 2 * FB :] = down[:, q * FB : (q + 1) * FB]


def grads(own, sib, hid, hid_t, a, b, weight, x_t, wd):
    whole = lambda shape: pl.BlockSpec(shape, lambda j: (0,) * len(shape))
    wide = pl.BlockSpec((ROWS, FB), lambda j: (0, j))
    return pl.pallas_call(
        grads_kernel,
        grid=(NFB,),
        out_shape=(
            jax.ShapeDtypeStruct((D, 3 * FF), bf16),
            jax.ShapeDtypeStruct((ROWS, FF), bf16),
            jax.ShapeDtypeStruct((ROWS, FF), bf16),
            jax.ShapeDtypeStruct((ROWS, META), f32),
        ),
        in_specs=[
            whole((HALF, D)), whole((HALF, D)), wide,
            pl.BlockSpec((FB, ROWS), lambda j: (j, 0)), wide, wide,
            whole((ROWS, META)), whole((D, ROWS)),
            pl.BlockSpec((FB, D), lambda j: (j, 0)),
        ],
        out_specs=(
            pl.BlockSpec((D, 3 * FB), lambda j: (0, j)), wide, wide, whole((ROWS, META)),
        ),
        scratch_shapes=[pltpu.VMEM((ROWS, D), bf16), pltpu.VMEM((ROWS, D), bf16)],
        compiler_params=pltpu.CompilerParams(vmem_limit_bytes=VLIM),
        name="grads",
    )(own, sib, hid, hid_t, a, b, weight, x_t, wd)


def slots_kernel(me_ref, gg_ref, gu_ref, route_ref, wg_ref, wu_ref, out_ref):
    me = me_ref[0]
    core = me % NC
    z = (me // NC) % NZ
    y = me // (NC * NZ)
    part = dot(gg_ref[...], wg_ref[...], contract_last)
    part = part + dot(gu_ref[...], wu_ref[...], contract_last)
    for h in range(2):
        for b in range(NY):
            for s in range(NZ):
                src = ((y + DY[b] + NY) % NY) * NZ + (z + DZ[s] + NZ) % NZ
                to = src * NC + (core if h == 0 else 1 - core)
                at = h * HALF + b * 64 + s * CAP
                out_ref[to, :, :D] = part[at : at + CAP].astype(bf16)
                out_ref[to, :, D:] = route_ref[at : at + CAP, :].astype(bf16)


def slots(me, gg, gu, route, wg, wu):
    return pl.pallas_call(
        slots_kernel,
        out_shape=jax.ShapeDtypeStruct((NY * NZ * NC, CAP, DA), bf16),
        in_specs=[SM] + [VM] * 5,
        out_specs=VM,
        compiler_params=pltpu.CompilerParams(vmem_limit_bytes=VLIM),
        name="slots",
    )(me, gg, gu, route, wg, wu)


def body(tokens, cotangent, expert_ids, route_weights, w_gate, w_up, w_down):
    me = lax.axis_index("ep").astype(i32).reshape(1)
    meta = jnp.concatenate(
        [expert_ids.astype(bf16), route_weights, jnp.zeros((TOK, META - 2 * TOPK), bf16)], axis=1
    )
    xa = jnp.concatenate([tokens, meta], axis=1)

    c1 = shift(cotangent, dy=1)
    c2 = shift(cotangent, dy=-1)
    c3 = shift(c1, dy=1)
    cot0 = jnp.concatenate([cotangent, c1, c2, c3], axis=0)

    u = [xa]
    d = [xa]
    for _ in range(3):
        u.append(shift(u[-1], dz=1))
        d.append(shift(d[-1], dz=-1))
    u.append(shift(u[-1], dz=1))
    x0 = jnp.concatenate(u + d[1:], axis=0)
    p1 = shift(x0, dy=1)
    m1 = shift(x0, dy=-1)
    n = NZ * TOK // 2
    qa = shift(p1[:n], dy=1)
    qb = shift(m1[n:], dy=-1)

    cu = [cot0]
    cd = [cot0]
    for _ in range(3):
        cu.append(shift(cu[-1], dz=1))
        cd.append(shift(cd[-1], dz=-1))
    n = NY * TOK // 2
    cq = [shift(cu[-1][:n], dz=1), shift(cd[-1][n:], dz=-1)]

    own_x, sib_x, code = pick_x(me, [x0, p1, m1, qa, qb])
    sib_x = swap_core(sib_x)
    wg, wu, wd = w_gate[0], w_up[0], w_down[0]
    hid, hid_t, a, b, weight, x_t = front(me, own_x, sib_x, wg, wu)

    own_c, sib_c = pick_cot(code, cu + cq + cd[1:])
    sib_c = swap_core(sib_c)
    grad, gg, gu, route = grads(own_c, sib_c, hid, hid_t, a, b, weight, x_t, wd)

    total = lax.psum_scatter(grad, "dp", scatter_dimension=0, tiled=True)
    out = slots(me, gg, gu, route, wg, wu)
    got = lax.all_to_all(out, "ep", split_axis=0, concat_axis=0, tiled=True)

    experts = NY * NZ * NC
    one = (expert_ids[:, :, None] == jnp.arange(experts, dtype=i32)).astype(i32)
    named = jnp.sum(one, axis=1)
    token = jnp.arange(TOK, dtype=i32)
    lower = (token[None, :] < token[:, None]).astype(bf16)
    earlier = dot(lower, named.astype(bf16)).astype(i32)
    row = jnp.arange(experts * CAP, dtype=i32)
    code_of = jnp.repeat(jnp.where(named > 0, earlier, -1), CAP, axis=1)
    sel = code_of == (row % CAP)[None, :]
    got = got.reshape(experts * CAP, DA)
    grad_tokens = dot(sel.astype(bf16), got[:, :D]).astype(bf16)
    mine = sel[:, None, :] & (expert_ids[:, :, None] == (row // CAP)[None, None, :])
    grad_route = jnp.sum(jnp.where(mine, got[:, D].astype(f32), 0.0), axis=2).astype(bf16)

    per = D // 4
    grad_gate = jnp.concatenate([total[:, j * FF : j * FF + FB] for j in range(NFB)], axis=1)
    grad_up = jnp.concatenate(
        [total[:, j * FF + FB : j * FF + 2 * FB] for j in range(NFB)], axis=1
    )
    grad_down = jnp.concatenate(
        [
            jnp.concatenate(
                [
                    total[q * FB : (q + 1) * FB, j * FF + 2 * FB : (j + 1) * FF]
                    for q in range(per // FB)
                ],
                axis=1,
            )
            for j in range(NFB)
        ],
        axis=0,
    )
    return grad_tokens, grad_route, grad_gate[None], grad_up[None], grad_down[None]


def solution(mesh):
    row = P(("ep", "dp"), None)
    expert = P("ep", None, None)
    return jax.shard_map(
        body,
        mesh=mesh,
        in_specs=(row, row, row, row, expert, expert, expert),
        out_specs=(row, row, P("ep", "dp", None), P("ep", "dp", None), P("ep", None, "dp")),
        check_vma=False,
    )
```

time: 414 us -> 231 us (0.56)
  local copies, waits for them, and re-layouts: 94.7 us -> 11.6 us
  blocking collectives: 61.6 us -> 0 us
  Pallas kernels: 0 us -> 44.4 us
  matrix products: 32 us -> 1.35 us
  other arithmetic: 32.4 us -> 3.43 us
  waiting for transfers between devices: 123 us -> 110 us
  starting transfers between devices: 53.6 us -> 45.3 us
    all_to_all x1 -> x0, blocking collectives: 61.6 us -> none  [body(): lax.all_to_all(send_x, 'ep', split_axis=0, concat_axis=0, tiled=True)]
    all_to_all x4 -> x1, starting transfers between devices: 53.4 us -> 6.24 us  [body(): got = lax.all_to_all(out, 'ep', split_axis=0, concat_axis=0, tiled=True)]
    pallas_call x0 -> x5, Pallas kernels: none -> 44.4 us  [the longest x1 16.1 us: grads(): pl.pallas_call(grads_kernel, grid=(NFB,), out_shape=(jax.ShapeDtypeStruct...]
    all_to_all x4 -> x1, waiting for transfers between devices: 92.5 us -> 53.1 us  [body(): got = lax.all_to_all(out, 'ep', split_axis=0, concat_axis=0, tiled=True)]
    ppermute x0 -> x24, starting transfers between devices: none -> 39 us  [the longest x22 33.2 us: shift(): return lax.ppermute(arr, 'ep', pairs)]
    ppermute x0 -> x24, waiting for transfers between devices: none -> 38.9 us  [the longest x22 38.9 us: shift(): return lax.ppermute(arr, 'ep', pairs)]
    gather x10 -> x0, local copies, waits for them, and re-layouts: 36.2 us -> none  [the longest x1 11.3 us: body(): packed = jnp.take(recv_joined, anchor, axis=0, mode='fill', fill_value=0)]
    while x90 -> x0, local copies, waits for them, and re-layouts: 32.2 us -> none
  transfers between devices with their start and end apart: 7 -> 26, of which waited for: 4 -> 11; matrix products, arithmetic and copies ran while one was open for 12% -> 3% of each run, Pallas kernels for 0% -> 12%
where the time goes in v1:
time: 231 us; the launch traced here: 230 us
  waiting for transfers between devices  110 us (48%)
  starting transfers between devices  45.3 us (20%)
  Pallas kernels  44.4 us (19%)
  between operations  14.3 us (6%)
  local copies, waits for them, and re-layouts  11.6 us (5%)
  other arithmetic  3.43 us (1%)
    all_to_all x1, waiting for transfers between devices, body(): got = lax.all_to_all(out, 'ep', split_axis=0, concat_axis=0, tiled=True)  53.1 us
    ppermute x22, waiting for transfers between devices, shift(): return lax.ppermute(arr, 'ep', pairs)  38.9 us
    ppermute x22, starting transfers between devices, shift(): return lax.ppermute(arr, 'ep', pairs)  33.2 us
    reduce_scatter x1, waiting for transfers between devices, body(): total = lax.psum_scatter(grad, 'dp', scatter_dimension=0, tiled=True)  17.8 us
    pallas_call x1, Pallas kernels, grads(): pl.pallas_call(grads_kernel, grid=(NFB,), out_shape=(jax.ShapeDtypeStruct...  16.1 us
    pallas_call x1, Pallas kernels, front(): pl.pallas_call(front_kernel, grid=(NFB,), out_shape=(jax.ShapeDtypeStruct...  9.25 us
    pallas_call x1, Pallas kernels, slots(): pl.pallas_call(slots_kernel, out_shape=jax.ShapeDtypeStruct((NY * NZ * NC...  8.31 us
    all_to_all x1, starting transfers between devices, body(): got = lax.all_to_all(out, 'ep', split_axis=0, concat_axis=0, tiled=True)  6.24 us
  transfers between devices with their start and end apart: 26, of which 11 were waited for; matrix products, arithmetic and copies ran while one was open for 3% of the time, Pallas kernels for 12%

profile of v1, /device:TPU:1, one launch (start us, length us, event | category | flops | bytes accessed | tf_op | source)
XLA Modules:
  0.0 230.3 jit_solution(13398687118369062745)
XLA Ops:
  9.8 2.5 %collective-permute-start = (bf16[32,2176]{1,0:T(8,128)(2,1)S(1)}, bf16[32,2176]{1,0:T(8,128)(2,1)S(1)}, u32[]{:S(2)}, u32[]{:S(2)}) collective-permute-start(bf16[32,2176]{1,0:T(8,128)(2,1)S(1)} %concatenate.27), channel_id=1, source_target_pairs={{0,8},{4,12},{8,16},{12,20},{16,24},{20,28},{24,32},{28,36},{32,40... | collective-permute-start | bytes 417800 | tf_op jit(solution)/shard_map/ppermute | solution.py:48
  12.3 4.0 %collective-permute-start.4 = (bf16[32,2176]{1,0:T(8,128)(2,1)S(1)}, bf16[32,2176]{1,0:T(8,128)(2,1)S(1)}, u32[]{:S(2)}, u32[]{:S(2)}) collective-permute-start(bf16[32,2176]{1,0:T(8,128)(2,1)S(1)} %concatenate.27), channel_id=1, source_target_pairs={{0,56},{4,60},{8,0},{12,4},{16,8},{20,12},{24,16},{28,20},{32,24},... | collective-permute-start | bytes 417800 | tf_op jit(solution)/shard_map/ppermute | solution.py:48
  22.1 2.7 %collective-permute-start.5 = (bf16[32,2176]{1,0:T(8,128)(2,1)S(1)}, bf16[32,2176]{1,0:T(8,128)(2,1)S(1)}, u32[]{:S(2)}, u32[]{:S(2)}) collective-permute-start(bf16[32,2176]{1,0:T(8,128)(2,1)S(1)} %collective-permute-done.4), channel_id=1, source_target_pairs={{0,56},{4,60},{8,0},{12,4},{16,8},{20,12},{24,16},{28,20},{32,24},... | collective-permute-start | bytes 417800 | tf_op jit(solution)/shard_map/ppermute | solution.py:48
  26.8 2.7 %collective-permute-start.18 = (bf16[128,2048]{1,0:T(8,128)(2,1)S(1)}, bf16[128,2048]{1,0:T(8,128)(2,1)S(1)}, u32[]{:S(2)}, u32[]{:S(2)}) collective-permute-start(bf16[128,2048]{1,0:T(8,128)(2,1)S(1)} %constant_dynamic-update-slice_fusion.8.refs_0_), channel_id=1, source_target_pairs={{0,56},{4,60},{8,0},{12,4},{16,8},{20,12},{24,16},{28,20},{32,24},... | collective-permute-start | bytes 1572872 | tf_op jit(solution)/shard_map/ppermute | solution.py:48
  29.5 2.7 %collective-permute-start.6 = (bf16[32,2176]{1,0:T(8,128)(2,1)S(1)}, bf16[32,2176]{1,0:T(8,128)(2,1)S(1)}, u32[]{:S(2)}, u32[]{:S(2)}) collective-permute-start(bf16[32,2176]{1,0:T(8,128)(2,1)S(1)} %collective-permute-done.5), channel_id=1, source_target_pairs={{0,56},{4,60},{8,0},{12,4},{16,8},{20,12},{24,16},{28,20},{32,24},... | collective-permute-start | bytes 417800 | tf_op jit(solution)/shard_map/ppermute | solution.py:48
  32.2 8.9 %collective-permute-done.2 = bf16[32,2176]{1,0:T(8,128)(2,1)S(1)} collective-permute-done((bf16[32,2176]{1,0:T(8,128)(2,1)S(1)}, bf16[32,2176]{1,0:T(8,128)(2,1)S(1)}, u32[]{:S(2)}, u32[]{:S(2)}) %collective-permute-start.2) | collective-permute-done | bytes 139296 | tf_op jit(solution)/shard_map/ppermute | solution.py:48
  41.2 5.1 %collective-permute-done.3 = bf16[32,2176]{1,0:T(8,128)(2,1)S(1)} collective-permute-done((bf16[32,2176]{1,0:T(8,128)(2,1)S(1)}, bf16[32,2176]{1,0:T(8,128)(2,1)S(1)}, u32[]{:S(2)}, u32[]{:S(2)}) %collective-permute-start.3) | collective-permute-done | bytes 139296 | tf_op jit(solution)/shard_map/ppermute | solution.py:48
  46.4 3.8 %collective-permute-start.8 = (bf16[256,2176]{1,0:T(8,128)(2,1)S(1)}, bf16[256,2176]{1,0:T(8,128)(2,1)S(1)}, u32[]{:S(2)}, u32[]{:S(2)}) collective-permute-start(bf16[256,2176]{1,0:T(8,128)(2,1)S(1)} %constant_dynamic-update-slice_fusion.b0), channel_id=1, source_target_pairs={{0,192},{4,196},{8,200},{12,204},{16,208},{20,212},{24,216},{28,22... | collective-permute-start | bytes 3342344 | tf_op jit(solution)/shard_map/ppermute | solution.py:48
  50.3 2.6 %collective-permute-start.19 = (bf16[128,2048]{1,0:T(8,128)(2,1)S(1)}, bf16[128,2048]{1,0:T(8,128)(2,1)S(1)}, u32[]{:S(2)}, u32[]{:S(2)}) collective-permute-start(bf16[128,2048]{1,0:T(8,128)(2,1)S(1)} %collective-permute-done.18.refs_6_), channel_id=1, source_target_pairs={{0,56},{4,60},{8,0},{12,4},{16,8},{20,12},{24,16},{28,20},{32,24},... | collective-permute-start | bytes 1572872 | tf_op jit(solution)/shard_map/ppermute | solution.py:48
  52.9 8.1 %collective-permute-done.15.refs_2_ = bf16[128,2048]{1,0:T(8,128)(2,1)S(1)} collective-permute-done((bf16[128,2048]{1,0:T(8,128)(2,1)S(1)}, bf16[128,2048]{1,0:T(8,128)(2,1)S(1)}, u32[]{:S(2)}, u32[]{:S(2)}) %collective-permute-start.15) | collective-permute-done | bytes 524320 | tf_op jit(solution)/shard_map/ppermute | solution.py:48
  61.1 2.7 %collective-permute-start.20 = (bf16[128,2048]{1,0:T(8,128)(2,1)S(1)}, bf16[128,2048]{1,0:T(8,128)(2,1)S(1)}, u32[]{:S(2)}, u32[]{:S(2)}) collective-permute-start(bf16[128,2048]{1,0:T(8,128)(2,1)S(1)} %collective-permute-done.19.refs_7_), channel_id=1, source_target_pairs={{0,56},{4,60},{8,0},{12,4},{16,8},{20,12},{24,16},{28,20},{32,24},... | collective-permute-start | bytes 1572872 | tf_op jit(solution)/shard_map/ppermute | solution.py:48
  63.8 6.7 %collective-permute-done.8.b2 = bf16[256,2176]{1,0:T(8,128)(2,1)S(1)} collective-permute-done((bf16[256,2176]{1,0:T(8,128)(2,1)S(1)}, bf16[256,2176]{1,0:T(8,128)(2,1)S(1)}, u32[]{:S(2)}, u32[]{:S(2)}) %collective-permute-start.8) | collective-permute-done | bytes 1114144 | tf_op jit(solution)/shard_map/ppermute | solution.py:48
  71.4 3.4 %collective-permute-start.10 = (bf16[128,2176]{1,0:T(8,128)(2,1)}, bf16[128,2176]{1,0:T(8,128)(2,1)}, u32[]{:S(2)}, u32[]{:S(2)}) collective-permute-start(bf16[128,2176]{1,0:T(8,128)(2,1)} %slice.73), channel_id=1, source_target_pairs={{0,192},{4,196},{8,200},{12,204},{16,208},{20,212},{24,216},{28,22... | collective-permute-start | bytes 1671176 | tf_op jit(solution)/shard_map/ppermute | solution.py:48
  77.3 2.7 %collective-permute-start.21 = (bf16[64,2048]{1,0:T(8,128)(2,1)}, bf16[64,2048]{1,0:T(8,128)(2,1)}, u32[]{:S(2)}, u32[]{:S(2)}) collective-permute-start(bf16[64,2048]{1,0:T(8,128)(2,1)} %slice.75), channel_id=1, source_target_pairs={{0,56},{4,60},{8,0},{12,4},{16,8},{20,12},{24,16},{28,20},{32,24},... | collective-permute-start | bytes 786440 | tf_op jit(solution)/shard_map/ppermute | solution.py:48
  82.5 4.0 %collective-permute-done.9.b3a = bf16[128,2176]{1,0:T(8,128)(2,1)} collective-permute-done((bf16[128,2176]{1,0:T(8,128)(2,1)}, bf16[128,2176]{1,0:T(8,128)(2,1)}, u32[]{:S(2)}, u32[]{:S(2)}) %collective-permute-start.9) | collective-permute-done | bytes 557088 | tf_op jit(solution)/shard_map/ppermute | solution.py:48
  86.5 5.9 %pick_x.1 = (bf16[256,2176]{1,0:T(8,128)(2,1)}, bf16[256,2176]{1,0:T(8,128)(2,1)}, bf16[4,256,128]{2,1,0:T(8,128)(2,1)}) custom-call(s32[1]{0:T(128)} %bitcast.1.me_ref, bf16[256,2176]{1,0:T(8,128)(2,1)} %copy-done.3, bf16[256,2176]{1,0:T(8,128)(2,1)} %copy-done.1, bf16[256,2176]{1,0:T(8,128)(2,1)} %copy-done, bf16[128,2176]{1,0:T(8,128)(2,1)} %collective-permute-done.9.b3a, ...), custom_call_target="tpu_custom_call" | custom-call | tf_op jit(solution)/shard_map/pick_x/pallas_call | solution.py:94
  92.4 5.8 %collective-permute-start.23 = (bf16[256,2176]{1,0:T(8,128)(2,1)}, bf16[256,2176]{1,0:T(8,128)(2,1)S(1)}, u32[]{:S(2)}, u32[]{:S(2)}) collective-permute-start(bf16[256,2176]{1,0:T(8,128)(2,1)} %get-tuple-element.24), channel_id=1, source_target_pairs={{0,4},{4,0},{8,12},{12,8},{16,20},{20,16},{24,28},{28,24},{32,36},... | collective-permute-start | bytes 3342344 | tf_op jit(solution)/shard_map/ppermute | solution.py:52
  98.9 4.9 %pick_cot.1 = (bf16[256,2048]{1,0:T(8,128)(2,1)}, bf16[256,2048]{1,0:T(8,128)(2,1)}) custom-call(bf16[4,256,128]{2,1,0:T(8,128)(2,1)} %get-tuple-element.20.code_ref, bf16[128,2048]{1,0:T(8,128)(2,1)} %copy-done.8, bf16[128,2048]{1,0:T(8,128)(2,1)} %copy-done.9, bf16[128,2048]{1,0:T(8,128)(2,1)} %copy-done.11, bf16[128,2048]{1,0:T(8,128)(2,1)} %copy-done.4, ...), custom_call_target="tpu_custom_call" | custom-call | tf_op jit(solution)/shard_map/pick_cot/pallas_call | solution.py:138
  104.8 9.3 %front.1 = (bf16[512,768]{1,0:T(8,128)(2,1)}, bf16[768,512]{1,0:T(8,128)(2,1)}, f32[512,768]{1,0:T(8,128)}, f32[512,768]{1,0:T(8,128)}, f32[512,128]{1,0:T(8,128)}, /*index=5*/bf16[2048,512]{1,0:T(8,128)(2,1)}) custom-call(s32[1]{0:T(128)} %bitcast.1.me_ref, bf16[256,2176]{1,0:T(8,128)(2,1)} %get-tuple-element.23.own_ref, bf16[256,2176]{1,0:T(8,128)(2,1)} %copy-done.6, ...), custom_call_target="tpu_custom_call" | custom-call | tf_op jit(solution)/shard_map/front/pallas_call | solution.py:185
  115.1 16.1 %grads.1 = (bf16[2048,2304]{1,0:T(8,128)(2,1)}, bf16[512,768]{1,0:T(8,128)(2,1)}, bf16[512,768]{1,0:T(8,128)(2,1)}, f32[512,128]{1,0:T(8,128)}) custom-call(bf16[256,2048]{1,0:T(8,128)(2,1)} %get-tuple-element.21.own_ref, bf16[256,2048]{1,0:T(8,128)(2,1)} %copy-done.7, bf16[512,768]{1,0:T(8,128)(2,1)} %get-tuple-element.25.hid_ref, ...), custom_call_target="tpu_custom_call" | custom-call | tf_op jit(solution)/shard_map/grads/pallas_call | solution.py:243
  131.2 8.3 %slots.1 = bf16[64,8,2176]{2,1,0:T(8,128)(2,1)} custom-call(s32[1]{0:T(128)} %bitcast.1.me_ref, bf16[512,768]{1,0:T(8,128)(2,1)} %get-tuple-element.31.gg_ref, bf16[512,768]{1,0:T(8,128)(2,1)} %get-tuple-element.32.gu_ref, f32[512,128]{1,0:T(8,128)} %get-tuple-element.33.route_ref, bf16[2048,768]{1,0:T(8,128)(2,1)} %bitcast.16, bf16[2048,768]{1,0:T(8,128)(2,1)} %bitcast.18), custom_call_target="tpu_custom_call" | custom-call | tf_op jit(solution)/shard_map/slots/pallas_call | solution.py:285
  139.5 6.2 %all-to-all-start = ((bf16[64,8,2176]{2,1,0:T(8,128)(2,1)}), bf16[64,8,2176]{2,1,0:T(8,128)(2,1)S(1)}, u32[]{:S(2)}, u32[]{:S(2)}) async-start(bf16[64,8,2176]{2,1,0:T(8,128)(2,1)} %slots.1), calls=%async_computation | async-start | bytes 4456448 | tf_op jit(solution)/shard_map/all_to_all | solution.py:339
  146.5 53.1 %all-to-all-done = bf16[64,8,2176]{2,1,0:T(8,128)(2,1)S(1)} async-done(((bf16[64,8,2176]{2,1,0:T(8,128)(2,1)}), bf16[64,8,2176]{2,1,0:T(8,128)(2,1)S(1)}, u32[]{:S(2)}, u32[]{:S(2)}) %all-to-all-start) | async-done | bytes 2228256 | tf_op jit(solution)/shard_map/all_to_all | solution.py:339
  201.9 17.8 %reduce-scatter.2.cloned.1.call-done = bf16[512,2304]{1,0:T(8,128)(2,1)} async-done(((bf16[2048,2304]{1,0:T(8,128)(2,1)}), bf16[512,2304]{1,0:T(8,128)(2,1)}) %reduce-scatter.2.cloned.1.call-update) | async-done | bytes 2359312 | tf_op jit(solution)/shard_map/reduce_scatter | solution.py:337
  (102 shorter events, 25.8 us)
Async XLA Ops:
  7.2 212.6 %reduce-scatter.2.cloned.1.call-start = ((), (), s32[]{:S(2)}) async-start(), calls=%async_computation.2 | async-start | bytes 11796480 | tf_op jit(solution)/shard_map/reduce_scatter | solution.py:337
  9.8 12.2 %collective-permute-start = (bf16[32,2176]{1,0:T(8,128)(2,1)S(1)}, bf16[32,2176]{1,0:T(8,128)(2,1)S(1)}, u32[]{:S(2)}, u32[]{:S(2)}) collective-permute-start(bf16[32,2176]{1,0:T(8,128)(2,1)S(1)} %concatenate.27), channel_id=1, source_target_pairs={{0,8},{4,12},{8,16},{12,20},{16,24},{20,28},{24,32},{28,36},{32,40... | collective-permute-start | bytes 417800 | tf_op jit(solution)/shard_map/ppermute | solution.py:48
  12.3 9.8 %collective-permute-start.4 = (bf16[32,2176]{1,0:T(8,128)(2,1)S(1)}, bf16[32,2176]{1,0:T(8,128)(2,1)S(1)}, u32[]{:S(2)}, u32[]{:S(2)}) collective-permute-start(bf16[32,2176]{1,0:T(8,128)(2,1)S(1)} %concatenate.27), channel_id=1, source_target_pairs={{0,56},{4,60},{8,0},{12,4},{16,8},{20,12},{24,16},{28,20},{32,24},... | collective-permute-start | bytes 417800 | tf_op jit(solution)/shard_map/ppermute | solution.py:48
  16.3 5.3 %collective-permute-start.11 = (bf16[32,2048]{1,0:T(8,128)(2,1)}, bf16[32,2048]{1,0:T(8,128)(2,1)S(1)}, u32[]{:S(2)}, u32[]{:S(2)}) collective-permute-start(bf16[32,2048]{1,0:T(8,128)(2,1)} %param.8), channel_id=1, source_target_pairs={{0,64},{4,68},{8,72},{12,76},{16,80},{20,84},{24,88},{28,92},{32,9... | collective-permute-start | bytes 393224 | tf_op jit(solution)/shard_map/ppermute | solution.py:48
  22.0 7.5 %collective-permute-start.1 = (bf16[32,2176]{1,0:T(8,128)(2,1)S(1)}, bf16[32,2176]{1,0:T(8,128)(2,1)S(1)}, u32[]{:S(2)}, u32[]{:S(2)}) collective-permute-start(bf16[32,2176]{1,0:T(8,128)(2,1)S(1)} %collective-permute-done), channel_id=1, source_target_pairs={{0,8},{4,12},{8,16},{12,20},{16,24},{20,28},{24,32},{28,36},{32,40... | collective-permute-start | bytes 417800 | tf_op jit(solution)/shard_map/ppermute | solution.py:48
  22.1 7.4 %collective-permute-start.5 = (bf16[32,2176]{1,0:T(8,128)(2,1)S(1)}, bf16[32,2176]{1,0:T(8,128)(2,1)S(1)}, u32[]{:S(2)}, u32[]{:S(2)}) collective-permute-start(bf16[32,2176]{1,0:T(8,128)(2,1)S(1)} %collective-permute-done.4), channel_id=1, source_target_pairs={{0,56},{4,60},{8,0},{12,4},{16,8},{20,12},{24,16},{28,20},{32,24},... | collective-permute-start | bytes 417800 | tf_op jit(solution)/shard_map/ppermute | solution.py:48
  26.7 23.5 %collective-permute-start.14 = (bf16[128,2048]{1,0:T(8,128)(2,1)S(1)}, bf16[128,2048]{1,0:T(8,128)(2,1)S(1)}, u32[]{:S(2)}, u32[]{:S(2)}) collective-permute-start(bf16[128,2048]{1,0:T(8,128)(2,1)S(1)} %constant_dynamic-update-slice_fusion.8.refs_0_), channel_id=1, source_target_pairs={{0,8},{4,12},{8,16},{12,20},{16,24},{20,28},{24,32},{28,36},{32,40... | collective-permute-start | bytes 1572872 | tf_op jit(solution)/shard_map/ppermute | solution.py:48
  26.8 23.5 %collective-permute-start.18 = (bf16[128,2048]{1,0:T(8,128)(2,1)S(1)}, bf16[128,2048]{1,0:T(8,128)(2,1)S(1)}, u32[]{:S(2)}, u32[]{:S(2)}) collective-permute-start(bf16[128,2048]{1,0:T(8,128)(2,1)S(1)} %constant_dynamic-update-slice_fusion.8.refs_0_), channel_id=1, source_target_pairs={{0,56},{4,60},{8,0},{12,4},{16,8},{20,12},{24,16},{28,20},{32,24},... | collective-permute-start | bytes 1572872 | tf_op jit(solution)/shard_map/ppermute | solution.py:48
  29.4 11.7 %collective-permute-start.2 = (bf16[32,2176]{1,0:T(8,128)(2,1)S(1)}, bf16[32,2176]{1,0:T(8,128)(2,1)S(1)}, u32[]{:S(2)}, u32[]{:S(2)}) collective-permute-start(bf16[32,2176]{1,0:T(8,128)(2,1)S(1)} %collective-permute-done.1), channel_id=1, source_target_pairs={{0,8},{4,12},{8,16},{12,20},{16,24},{20,28},{24,32},{28,36},{32,40... | collective-permute-start | bytes 417800 | tf_op jit(solution)/shard_map/ppermute | solution.py:48
  29.5 16.8 %collective-permute-start.6 = (bf16[32,2176]{1,0:T(8,128)(2,1)S(1)}, bf16[32,2176]{1,0:T(8,128)(2,1)S(1)}, u32[]{:S(2)}, u32[]{:S(2)}) collective-permute-start(bf16[32,2176]{1,0:T(8,128)(2,1)S(1)} %collective-permute-done.5), channel_id=1, source_target_pairs={{0,56},{4,60},{8,0},{12,4},{16,8},{20,12},{24,16},{28,20},{32,24},... | collective-permute-start | bytes 417800 | tf_op jit(solution)/shard_map/ppermute | solution.py:48
  41.1 5.1 %collective-permute-start.3 = (bf16[32,2176]{1,0:T(8,128)(2,1)S(1)}, bf16[32,2176]{1,0:T(8,128)(2,1)S(1)}, u32[]{:S(2)}, u32[]{:S(2)}) collective-permute-start(bf16[32,2176]{1,0:T(8,128)(2,1)S(1)} %collective-permute-done.2), channel_id=1, source_target_pairs={{0,8},{4,12},{8,16},{12,20},{16,24},{20,28},{24,32},{28,36},{32,40... | collective-permute-start | bytes 417800 | tf_op jit(solution)/shard_map/ppermute | solution.py:48
  46.4 24.1 %collective-permute-start.8 = (bf16[256,2176]{1,0:T(8,128)(2,1)S(1)}, bf16[256,2176]{1,0:T(8,128)(2,1)S(1)}, u32[]{:S(2)}, u32[]{:S(2)}) collective-permute-start(bf16[256,2176]{1,0:T(8,128)(2,1)S(1)} %constant_dynamic-update-slice_fusion.b0), channel_id=1, source_target_pairs={{0,192},{4,196},{8,200},{12,204},{16,208},{20,212},{24,216},{28,22... | collective-permute-start | bytes 3342344 | tf_op jit(solution)/shard_map/ppermute | solution.py:48
  50.2 24.6 %collective-permute-start.7 = (bf16[256,2176]{1,0:T(8,128)(2,1)S(1)}, bf16[256,2176]{1,0:T(8,128)(2,1)S(1)}, u32[]{:S(2)}, u32[]{:S(2)}) collective-permute-start(bf16[256,2176]{1,0:T(8,128)(2,1)S(1)} %constant_dynamic-update-slice_fusion.b0), channel_id=1, source_target_pairs={{0,64},{4,68},{8,72},{12,76},{16,80},{20,84},{24,88},{28,92},{32,9... | collective-permute-start | bytes 3342344 | tf_op jit(solution)/shard_map/ppermute | solution.py:48
  50.2 10.8 %collective-permute-start.15 = (bf16[128,2048]{1,0:T(8,128)(2,1)S(1)}, bf16[128,2048]{1,0:T(8,128)(2,1)S(1)}, u32[]{:S(2)}, u32[]{:S(2)}) collective-permute-start(bf16[128,2048]{1,0:T(8,128)(2,1)S(1)} %collective-permute-done.14.refs_1_), channel_id=1, source_target_pairs={{0,8},{4,12},{8,16},{12,20},{16,24},{20,28},{24,32},{28,36},{32,40... | collective-permute-start | bytes 1572872 | tf_op jit(solution)/shard_map/ppermute | solution.py:48
  50.3 10.7 %collective-permute-start.19 = (bf16[128,2048]{1,0:T(8,128)(2,1)S(1)}, bf16[128,2048]{1,0:T(8,128)(2,1)S(1)}, u32[]{:S(2)}, u32[]{:S(2)}) collective-permute-start(bf16[128,2048]{1,0:T(8,128)(2,1)S(1)} %collective-permute-done.18.refs_6_), channel_id=1, source_target_pairs={{0,56},{4,60},{8,0},{12,4},{16,8},{20,12},{24,16},{28,20},{32,24},... | collective-permute-start | bytes 1572872 | tf_op jit(solution)/shard_map/ppermute | solution.py:48
  61.0 14.6 %collective-permute-start.16 = (bf16[128,2048]{1,0:T(8,128)(2,1)S(1)}, bf16[128,2048]{1,0:T(8,128)(2,1)S(1)}, u32[]{:S(2)}, u32[]{:S(2)}) collective-permute-start(bf16[128,2048]{1,0:T(8,128)(2,1)S(1)} %collective-permute-done.15.refs_2_), channel_id=1, source_target_pairs={{0,8},{4,12},{8,16},{12,20},{16,24},{20,28},{24,32},{28,36},{32,40... | collective-permute-start | bytes 1572872 | tf_op jit(solution)/shard_map/ppermute | solution.py:48
  61.1 15.4 %collective-permute-start.20 = (bf16[128,2048]{1,0:T(8,128)(2,1)S(1)}, bf16[128,2048]{1,0:T(8,128)(2,1)S(1)}, u32[]{:S(2)}, u32[]{:S(2)}) collective-permute-start(bf16[128,2048]{1,0:T(8,128)(2,1)S(1)} %collective-permute-done.19.refs_7_), channel_id=1, source_target_pairs={{0,56},{4,60},{8,0},{12,4},{16,8},{20,12},{24,16},{28,20},{32,24},... | collective-permute-start | bytes 1572872 | tf_op jit(solution)/shard_map/ppermute | solution.py:48
  71.4 11.1 %collective-permute-start.10 = (bf16[128,2176]{1,0:T(8,128)(2,1)}, bf16[128,2176]{1,0:T(8,128)(2,1)}, u32[]{:S(2)}, u32[]{:S(2)}) collective-permute-start(bf16[128,2176]{1,0:T(8,128)(2,1)} %slice.73), channel_id=1, source_target_pairs={{0,192},{4,196},{8,200},{12,204},{16,208},{20,212},{24,216},{28,22... | collective-permute-start | bytes 1671176 | tf_op jit(solution)/shard_map/ppermute | solution.py:48
  75.7 10.9 %collective-permute-start.9 = (bf16[128,2176]{1,0:T(8,128)(2,1)}, bf16[128,2176]{1,0:T(8,128)(2,1)}, u32[]{:S(2)}, u32[]{:S(2)}) collective-permute-start(bf16[128,2176]{1,0:T(8,128)(2,1)} %slice.72), channel_id=1, source_target_pairs={{0,64},{4,68},{8,72},{12,76},{16,80},{20,84},{24,88},{28,92},{32,9... | collective-permute-start | bytes 1671176 | tf_op jit(solution)/shard_map/ppermute | solution.py:48
  76.5 21.8 %collective-permute-start.17 = (bf16[64,2048]{1,0:T(8,128)(2,1)}, bf16[64,2048]{1,0:T(8,128)(2,1)S(1)}, u32[]{:S(2)}, u32[]{:S(2)}) collective-permute-start(bf16[64,2048]{1,0:T(8,128)(2,1)} %slice.74), channel_id=1, source_target_pairs={{0,8},{4,12},{8,16},{12,20},{16,24},{20,28},{24,32},{28,36},{32,40... | collective-permute-start | bytes 786440 | tf_op jit(solution)/shard_map/ppermute | solution.py:48
  77.3 21.0 %collective-permute-start.21 = (bf16[64,2048]{1,0:T(8,128)(2,1)}, bf16[64,2048]{1,0:T(8,128)(2,1)}, u32[]{:S(2)}, u32[]{:S(2)}) collective-permute-start(bf16[64,2048]{1,0:T(8,128)(2,1)} %slice.75), channel_id=1, source_target_pairs={{0,56},{4,60},{8,0},{12,4},{16,8},{20,12},{24,16},{28,20},{32,24},... | collective-permute-start | bytes 786440 | tf_op jit(solution)/shard_map/ppermute | solution.py:48
  92.4 11.4 %collective-permute-start.23 = (bf16[256,2176]{1,0:T(8,128)(2,1)}, bf16[256,2176]{1,0:T(8,128)(2,1)S(1)}, u32[]{:S(2)}, u32[]{:S(2)}) collective-permute-start(bf16[256,2176]{1,0:T(8,128)(2,1)} %get-tuple-element.24), channel_id=1, source_target_pairs={{0,4},{4,0},{8,12},{12,8},{16,20},{20,16},{24,28},{28,24},{32,36},... | collective-permute-start | bytes 3342344 | tf_op jit(solution)/shard_map/ppermute | solution.py:52
  103.8 10.3 %collective-permute-start.22 = (bf16[256,2048]{1,0:T(8,128)(2,1)}, bf16[256,2048]{1,0:T(8,128)(2,1)S(1)}, u32[]{:S(2)}, u32[]{:S(2)}) collective-permute-start(bf16[256,2048]{1,0:T(8,128)(2,1)} %get-tuple-element.22), channel_id=1, source_target_pairs={{0,4},{4,0},{8,12},{12,8},{16,20},{20,16},{24,28},{28,24},{32,36},... | collective-permute-start | bytes 3145736 | tf_op jit(solution)/shard_map/ppermute | solution.py:52
  139.5 60.1 %all-to-all-start = ((bf16[64,8,2176]{2,1,0:T(8,128)(2,1)}), bf16[64,8,2176]{2,1,0:T(8,128)(2,1)S(1)}, u32[]{:S(2)}, u32[]{:S(2)}) async-start(bf16[64,8,2176]{2,1,0:T(8,128)(2,1)} %slots.1), calls=%async_computation | async-start | bytes 4456448 | tf_op jit(solution)/shard_map/all_to_all | solution.py:339
  (17 other events, 206.1 us)
Sparse Core Ops, SparseCore 0:
  131.4 88.3 reduce-scatter.1
